TPU v7x, 512 devices: a whole 4x8x8 slice. The times are simulated.
512 devices in a mesh: rep: 4 (over z_hi), dp: 16 (over y, core), tensor: 8 (over x, z_lo).
Axes of the slice: x: 4, y: 8, z: 8 (z_hi: 4, z_lo: 2; z = z_hi * 2 + z_lo), core: 2. Of those that a mesh axis runs over, the one named last changes fastest.
Arguments:
- grad_proj: float32 [64, 3072, 1536], P(('rep', 'dp'), 'tensor'), as said below
- grad_conv: float32 [64, 4, 3328], P(('rep', 'dp'), None, 'tensor'), may hold values from -24 to 24
- param_proj: float32 [3072, 1536], P('tensor', 'dp'), may hold values from -6 to 6
- m_proj: float32 [3072, 1536], P('tensor', 'dp'), may hold values from -2 to 2
- v_proj: float32 [3072, 1536], P('tensor', 'dp'), may hold values from 0.02 to 0.2
- ema_proj: float32 [3072, 1536], P(('tensor', 'dp')), may hold values from -6 to 6
- param_conv: float32 [4, 3328], P(None, 'tensor'), may hold values from -3 to 3
- m_conv: float32 [4, 3328], P(None, 'tensor'), may hold values from -2 to 2
- v_conv: float32 [4, 3328], P(None, 'tensor'), may hold values from 0.02 to 0.2
Outputs:
- new_param_proj: float32 [3072, 1536], P('tensor', 'dp')
- new_m_proj: float32 [3072, 1536], P('tensor', 'dp')
- new_v_proj: float32 [3072, 1536], P('tensor', 'dp')
- new_ema_proj: float32 [3072, 1536], P(('tensor', 'dp'))
- weights_proj: bfloat16 [3072, 1536], P('tensor')
- new_param_conv: float32 [4, 3328], P(None, 'tensor')
- new_m_conv: float32 [4, 3328], P(None, 'tensor')
- new_v_conv: float32 [4, 3328], P(None, 'tensor')
Inputs may be any that keep to these rules, and one draw needn't show every extreme that they name: `grad_proj`: Real-valued gradients with entries of magnitude below 3100.
All inputs are finite; a program needn't handle non-finite values.
Results may differ from a plain program's by a relative error of at most 0.001.
Values may be sent and summed in bfloat16 or wider, within the bound.
A program may use at most 64 MiB of HBM per device.

v0:
```python
import math
import jax
import jax.numpy as jnp
from jax import lax
from jax.sharding import PartitionSpec as P

D = 1536
INNER = 3072
CONV = 3328
KCONV = 4


def adamw_step(param_in, first_in, second_in, grad_in):
    first_out = 0.9 * first_in + 0.1 * grad_in
    second_out = 0.95 * second_in + 0.05 * grad_in * grad_in
    bias_one = 1.0 - 0.9**10
    bias_two = 1.0 - 0.95**10
    update = first_out / bias_one / (jnp.sqrt(second_out / bias_two) + 1e-08)
    param_out = param_in - 0.25 * (update + 0.1 * param_in)
    return (param_out, first_out, second_out)


def clip_from(square_sum):
    clip_limit = 0.5 * math.sqrt(INNER * D + KCONV * CONV)
    return jnp.minimum(1.0, clip_limit / (jnp.sqrt(square_sum) + 1e-06))


def body(grad_proj, grad_conv, param_proj, m_proj, v_proj, ema_proj, param_conv, m_conv, v_conv):
    replica_count = lax.axis_size("rep") * lax.axis_size("dp")
    conv_avg = lax.psum(grad_conv[0], ("rep", "dp")) / replica_count
    conv_square = jnp.sum(conv_avg * conv_avg)
    first_owner = lax.axis_index("dp") == 0
    owner_sum = lax.psum_scatter(grad_proj[0], "dp", scatter_dimension=1, tiled=True)
    proj_avg = lax.psum(owner_sum, "rep") / replica_count
    conv_share = jnp.where(first_owner, conv_square, jnp.float32(0.0))
    square_sum = lax.psum(jnp.sum(proj_avg * proj_avg) + conv_share, ("dp", "tensor"))
    clip_factor = clip_from(square_sum)
    new_param_proj, new_m_proj, new_v_proj = adamw_step(
        param_proj, m_proj, v_proj, clip_factor * proj_avg
    )
    new_param_conv, new_m_conv, new_v_conv = adamw_step(
        param_conv, m_conv, v_conv, clip_factor * conv_avg
    )
    ema_count = ema_proj.shape[0]
    full_block = lax.all_gather(
        new_param_proj.astype(jnp.bfloat16), "dp", axis=1, tiled=True
    ).astype(new_param_proj.dtype)
    weights_proj = full_block.astype(jnp.bfloat16)
    row_block = lax.dynamic_slice_in_dim(full_block, lax.axis_index("dp") * ema_count, ema_count, 0)
    new_ema_proj = 0.9 * ema_proj + 0.1 * row_block
    return (
        new_param_proj,
        new_m_proj,
        new_v_proj,
        new_ema_proj,
        weights_proj,
        new_param_conv,
        new_m_conv,
        new_v_conv,
    )


def solution(mesh):
    in_specs = (
        P(("rep", "dp"), "tensor", None),
        P(("rep", "dp"), None, "tensor"),
        P("tensor", "dp"),
        P("tensor", "dp"),
        P("tensor", "dp"),
        P(("tensor", "dp"), None),
        P(None, "tensor"),
        P(None, "tensor"),
        P(None, "tensor"),
    )
    out_specs = (
        P("tensor", "dp"),
        P("tensor", "dp"),
        P("tensor", "dp"),
        P(("tensor", "dp"), None),
        P("tensor", None),
        P(None, "tensor"),
        P(None, "tensor"),
        P(None, "tensor"),
    )
    return jax.shard_map(body, mesh=mesh, in_specs=in_specs, out_specs=out_specs, check_vma=False)
```

profile of v0, /device:TPU:1, one launch (start us, length us, event | category | flops | bytes accessed | tf_op | source)
XLA Modules:
  0.0 549.1 jit_solution(13845586338401462347)
XLA Ops:
  7.2 0.0 reduce-scatter.2.cloned.1.call-start
  7.2 3.1 copy.19
  10.3 0.0 copy-start.8
  10.3 0.0 copy-start.2
  10.3 0.0 copy-start.3
  10.3 0.0 copy-start.4
  10.3 0.0 reduce-scatter.2.cloned.1.call-update
  10.3 0.0 copy-start.1
  10.3 0.0 all-reduce.2.cloned.1.call-start
  10.4 66.1 %reduce-scatter.2.cloned.1.call-done = f32[384,96]{0,1:T(8,128)} async-done(((f32[384,1536]{0,1:T(8,128)}), f32[384,96]{0,1:T(8,128)}) %reduce-scatter.2.cloned.1.call-update) | async-done | bytes 147472 | tf_op jit(solution)/shard_map/reduce_scatter | solution.py:33
  76.5 0.0 all-reduce.2.cloned.1.call-update
  76.5 0.0 copy-start.5
  76.5 0.0 copy-start.6
  76.5 0.0 copy-start.7
  76.5 0.0 all-gather.2.cloned.1.call-start
  76.6 0.0 copy-done.8
  76.6 142.5 %psum.22 = f32[4,416]{1,0:T(4,128)S(1)} all-reduce(f32[4,416]{1,0:T(4,128)S(1)} %bitcast.3), channel_id=1, replica_groups=mesh['rep'=4,'dp'=16,'tensor'=8] {'rep','dp'}, use_global_device_ids=true, to_apply=%region_3.0 | all-reduce | flops 1664 | bytes 13312 | tf_op jit(solution)/shard_map/psum | solution.py:30
  219.1 0.6 multiply_reduce_fusion.1
  220.3 0.0 all-reduce.2.cloned.1.call-done
  220.4 1.6 multiply_reduce_fusion
  222.6 270.7 %psum.23 = f32[]{:T(128)} all-reduce(f32[]{:T(128)S(6)} %add.50), channel_id=1, replica_groups=mesh['rep'=4,'dp'=16,'tensor'=8] {'dp','tensor'}, use_global_device_ids=true, to_apply=%region_5.6 | all-reduce | flops 1 | bytes 8 | tf_op jit(solution)/shard_map/psum | solution.py:36
  494.0 0.0 copy-done.2
  494.0 0.0 copy-done.3
  494.0 0.0 copy-done.4
  494.0 1.8 fusion.3
  495.7 0.0 all-gather.2.cloned.1.call-update
  495.8 0.0 copy-done.1
  495.8 0.3 copy.20
  496.1 0.0 copy-done.5
  496.1 0.0 copy-done.6
  496.1 0.0 copy-done.7
  496.1 0.6 multiply_subtract_fusion.1
  496.7 42.1 %all-gather.2.cloned.1.call-done = bf16[384,1536]{0,1:T(8,128)(2,1)} async-done(((bf16[384,96]{0,1:T(8,128)(2,1)}), bf16[384,1536]{0,1:T(8,128)(2,1)}) %all-gather.2.cloned.1.call-update) | async-done | bytes 1179664 | tf_op jit(solution)/shard_map/all_gather | solution.py:45
  538.8 0.0 copy-start
  538.8 1.4 multiply_add_fusion
  540.3 0.9 copy.21
  541.2 0.0 copy-done
  541.2 1.4 copy.22
Async XLA Ops:
  7.2 69.3 %reduce-scatter.2.cloned.1.call-start = ((), (), s32[]{:S(2)}) async-start(), calls=%async_computation.1 | async-start | bytes 2506752 | tf_op jit(solution)/shard_map/reduce_scatter | solution.py:33
  10.3 66.3 %copy-start.8 = (f32[1,4,416]{2,1,0:T(4,128)S(1)}, f32[1,4,416]{2,1,0:T(4,128)}, u32[]{:S(2)}) copy-start(f32[1,4,416]{2,1,0:T(4,128)} %param.10) | copy-start | bytes 19972
  10.3 483.7 %copy-start.2 = (f32[384,96]{0,1:T(8,128)S(1)}, f32[384,96]{0,1:T(8,128)}, u32[]{:S(2)}) copy-start(f32[384,96]{0,1:T(8,128)} %param.11) | copy-start | bytes 442372
  10.3 483.7 %copy-start.3 = (f32[384,96]{0,1:T(8,128)S(1)}, f32[384,96]{0,1:T(8,128)}, u32[]{:S(2)}) copy-start(f32[384,96]{0,1:T(8,128)} %param.12) | copy-start | bytes 442372
  10.3 483.7 %copy-start.4 = (f32[384,96]{0,1:T(8,128)S(1)}, f32[384,96]{0,1:T(8,128)}, u32[]{:S(2)}) copy-start(f32[384,96]{0,1:T(8,128)} %param.13) | copy-start | bytes 442372
  10.3 485.4 %copy-start.1 = (f32[24,1536]{1,0:T(8,128)S(1)}, f32[24,1536]{1,0:T(8,128)}, u32[]{:S(2)}) copy-start(f32[24,1536]{1,0:T(8,128)} %param.14) | copy-start | bytes 442372
  10.3 210.0 %all-reduce.2.cloned.1.call-start = ((), (), s32[]{:S(2)}) async-start(), calls=%async_computation.2 | async-start | bytes 294912 | tf_op jit(solution)/shard_map/psum | solution.py:34
  76.5 419.6 %copy-start.5 = (f32[4,416]{1,0:T(4,128)S(1)}, f32[4,416]{1,0:T(4,128)}, u32[]{:S(2)}) copy-start(f32[4,416]{1,0:T(4,128)} %param.15) | copy-start | bytes 19972
  76.5 419.5 %copy-start.6 = (f32[4,416]{1,0:T(4,128)S(1)}, f32[4,416]{1,0:T(4,128)}, u32[]{:S(2)}) copy-start(f32[4,416]{1,0:T(4,128)} %param.16) | copy-start | bytes 19972
  76.5 419.5 %copy-start.7 = (f32[4,416]{1,0:T(4,128)S(1)}, f32[4,416]{1,0:T(4,128)}, u32[]{:S(2)}) copy-start(f32[4,416]{1,0:T(4,128)} %param.17) | copy-start | bytes 19972
  76.5 462.3 %all-gather.2.cloned.1.call-start = ((), (), s32[]{:S(2)}) async-start(), calls=%async_computation.3 | async-start | bytes 1253376 | tf_op jit(solution)/shard_map/all_gather | solution.py:45
  538.8 2.3 copy-start
Sparse Core Ops, SparseCore 0:
  10.8 65.6 reduce-scatter.1
  79.4 55.1 all-reduce.1
  495.9 42.8 all-gather.1
where the time goes:
time: 549 us
  blocking collectives  413 us (75%)
  waiting for transfers between devices  108 us (20%)
  between operations  15.9 us (3%)
  other arithmetic  5.98 us (1%)
  local copies, waits for them, and re-layouts  5.74 us (1%)
    psum x1, blocking collectives, body(): lax.psum(jnp.sum(proj_avg * proj_avg) + conv_share, ('dp', 'tensor'))  271 us
    psum x1, blocking collectives, body(): conv_avg = lax.psum(grad_conv[0], ('rep', 'dp')) / replica_count  142 us
    reduce_scatter x1, waiting for transfers between devices, body(): lax.psum_scatter(grad_proj[0], 'dp', scatter_dimension=1, tiled=True)  66.1 us
    all_gather x1, waiting for transfers between devices, body(): lax.all_gather(new_param_proj.astype(jnp.bfloat16), 'dp', axis=1, tiled=T...  42.1 us
  transfers between devices with their start and end apart: 3, of which 2 were waited for; matrix products, arithmetic and copies ran while one was open for 0% of the time, Pallas kernels for 0%

commit v1 on v0

--- a/solution.py
+++ b/solution.py
@@ -8,6 +8,22 @@
 INNER = 3072
 CONV = 3328
 KCONV = 4
+
+
+def tell_plate_all(arr, row_axis):
+    n_lanes = lax.axis_size(row_axis)
+    heap = [(it, (it + 1) % n_lanes) for it in range(n_lanes)]
+    shelf = [(it, (it - 1) % n_lanes) for it in range(n_lanes)]
+    local_part, clean = ([arr], [arr])
+    for _ in range(n_lanes // 2):
+        known = lax.ppermute(local_part[-1], row_axis, heap)
+        local_part.append(known)
+    for _ in range((n_lanes - 1) // 2):
+        aux = lax.ppermute(clean[-1], row_axis, shelf)
+        clean.append(aux)
+    tmp = jnp.concatenate([*local_part[::-1], *clean[1:]], axis=1)
+    current_value = lax.axis_index(row_axis)
+    return jnp.roll(tmp, shift=(current_value - n_lanes // 2) * arr.shape[1], axis=1)
 
 
 def adamw_step(param_in, first_in, second_in, grad_in):
@@ -42,9 +58,9 @@
         param_conv, m_conv, v_conv, clip_factor * conv_avg
     )
     ema_count = ema_proj.shape[0]
-    full_block = lax.all_gather(
-        new_param_proj.astype(jnp.bfloat16), "dp", axis=1, tiled=True
-    ).astype(new_param_proj.dtype)
+    full_block = tell_plate_all(new_param_proj.astype(jnp.bfloat16), "dp").astype(
+        new_param_proj.dtype
+    )
     weights_proj = full_block.astype(jnp.bfloat16)
     row_block = lax.dynamic_slice_in_dim(full_block, lax.axis_index("dp") * ema_count, ema_count, 0)
     new_ema_proj = 0.9 * ema_proj + 0.1 * row_block

time: 549 us -> 561 us (1.022)
  starting transfers between devices: 0.12 us -> 37.4 us
  waiting for transfers between devices: 108 us -> 76.6 us
    all_gather x1 -> x0, waiting for transfers between devices: 42.1 us -> none  [body(): lax.all_gather(new_param_proj.astype(jnp.bfloat16), 'dp', axis=1, tiled=T...]
    ppermute x0 -> x15, starting transfers between devices: none -> 37.3 us  [the longest x7 37.3 us: tell_plate_all(): aux = lax.ppermute(clean[-1], row_axis, shelf)]
    ppermute x0 -> x15, waiting for transfers between devices: none -> 10.5 us  [the longest x8 9.5 us: tell_plate_all(): known = lax.ppermute(local_part[-1], row_axis, heap)]
  transfers between devices with their start and end apart: 3 -> 17, of which waited for: 2 -> 15; matrix products, arithmetic and copies ran while one was open for 0% -> 0% of each run, Pallas kernels for 0% -> 0%
where the time goes in v1:
time: 561 us; the launch traced here: 558 us
  blocking collectives  413 us (74%)
  waiting for transfers between devices  76.6 us (14%)
  starting transfers between devices  37.4 us (7%)
  between operations  16.3 us (3%)
  local copies, waits for them, and re-layouts  9.7 us (2%)
    psum x1, blocking collectives, body(): lax.psum(jnp.sum(proj_avg * proj_avg) + conv_share, ('dp', 'tensor'))  270 us
    psum x1, blocking collectives, body(): conv_avg = lax.psum(grad_conv[0], ('rep', 'dp')) / replica_count  143 us
    reduce_scatter x1, waiting for transfers between devices, body(): lax.psum_scatter(grad_proj[0], 'dp', scatter_dimension=1, tiled=True)  66.1 us
    ppermute x7, starting transfers between devices, tell_plate_all(): aux = lax.ppermute(clean[-1], row_axis, shelf)  37.3 us
  transfers between devices with their start and end apart: 17, of which 15 were waited for; matrix products, arithmetic and copies ran while one was open for 0% of the time, Pallas kernels for 0%

profile of v1, /device:TPU:1, one launch (start us, length us, event | category | flops | bytes accessed | tf_op | source)
XLA Modules:
  0.0 558.2 jit_solution(11351160351054649460)
XLA Ops:
  7.2 0.0 reduce-scatter.2.cloned.1.call-start
  7.2 3.1 copy.17
  10.3 0.0 copy-start.10
  10.3 0.0 copy-start.11
  10.3 0.0 copy-start.12
  10.3 0.0 reduce-scatter.2.cloned.1.call-update
  10.4 0.0 all-reduce.2.cloned.1.call-start
  10.4 66.1 %reduce-scatter.2.cloned.1.call-done = f32[384,96]{0,1:T(8,128)} async-done(((f32[384,1536]{0,1:T(8,128)}), f32[384,96]{0,1:T(8,128)}) %reduce-scatter.2.cloned.1.call-update) | async-done | bytes 147472 | tf_op jit(solution)/shard_map/reduce_scatter | solution.py:49
  76.5 0.0 all-reduce.2.cloned.1.call-update
  76.5 142.5 %psum.22 = f32[4,416]{1,0:T(4,128)S(1)} all-reduce(f32[4,416]{1,0:T(4,128)S(1)} %bitcast.3), channel_id=1, replica_groups=mesh['rep'=4,'dp'=16,'tensor'=8] {'rep','dp'}, use_global_device_ids=true, to_apply=%region_3.0 | all-reduce | flops 1664 | bytes 13312 | tf_op jit(solution)/shard_map/psum | solution.py:46
  219.1 0.6 multiply_reduce_fusion.1
  220.3 0.0 all-reduce.2.cloned.1.call-done
  220.3 1.6 multiply_reduce_fusion
  222.5 270.5 %psum.23 = f32[]{:T(128)} all-reduce(f32[]{:T(128)S(6)} %add.61), channel_id=1, replica_groups=mesh['rep'=4,'dp'=16,'tensor'=8] {'dp','tensor'}, use_global_device_ids=true, to_apply=%region_5.6 | all-reduce | flops 1 | bytes 8 | tf_op jit(solution)/shard_map/psum | solution.py:52
  493.8 1.7 multiply_subtract_fusion
  495.5 0.1 copy.18
  495.7 0.0 collective-permute-start
  495.7 11.4 %collective-permute-start.8 = (bf16[384,96]{1,0:T(8,128)(2,1)S(1)}, bf16[384,96]{1,0:T(8,128)(2,1)S(1)}, u32[]{:S(2)}, u32[]{:S(2)}) collective-permute-start(bf16[384,96]{1,0:T(8,128)(2,1)S(1)} %copy.18), channel_id=1, source_target_pairs={{0,120},{8,0},{16,8},{24,16},{32,24},{40,32},{48,40},{56,48},{64,5... | collective-permute-start | bytes 221192 | tf_op jit(solution)/shard_map/ppermute | solution.py:22
  507.1 0.8 collective-permute-done
  507.9 0.0 collective-permute-start.1
  507.9 0.2 collective-permute-done.8
  508.0 4.3 collective-permute-start.9
  512.3 0.8 collective-permute-done.1
  513.1 0.0 collective-permute-start.2
  513.1 0.2 collective-permute-done.9
  513.3 4.3 collective-permute-start.10
  517.6 0.8 collective-permute-done.2
  518.4 0.0 collective-permute-start.3
  518.4 0.2 collective-permute-done.10
  518.5 4.3 collective-permute-start.11
  522.8 0.8 collective-permute-done.3
  523.6 0.0 collective-permute-start.4
  523.6 0.2 collective-permute-done.11
  523.8 4.3 collective-permute-start.12
  528.1 0.8 collective-permute-done.4
  528.9 0.2 collective-permute-done.12
  529.0 4.3 collective-permute-start.13
  533.4 0.8 collective-permute-done.5
  534.1 0.2 collective-permute-done.13
  534.3 4.3 collective-permute-start.14
  538.6 0.8 collective-permute-done.6
  539.4 0.6 multiply_subtract_fusion.1
  540.1 0.6 copy-done.5
  540.7 4.0 collective-permute-done.7
  544.8 4.2 concatenate.6
  549.0 0.0 copy-start.9
  549.1 1.6 constant_dynamic-slice_fusion
  550.6 0.8 multiply_add_fusion
  (27 shorter events, 0.1 us)
Async XLA Ops:
  7.2 69.3 %reduce-scatter.2.cloned.1.call-start = ((), (), s32[]{:S(2)}) async-start(), calls=%async_computation.1 | async-start | bytes 2506752 | tf_op jit(solution)/shard_map/reduce_scatter | solution.py:49
  10.3 66.2 %copy-start.13 = (f32[1,4,416]{2,1,0:T(4,128)S(1)}, f32[1,4,416]{2,1,0:T(4,128)}, u32[]{:S(2)}) copy-start(f32[1,4,416]{2,1,0:T(4,128)} %param.10) | copy-start | bytes 19972
  10.3 483.5 %copy-start.6 = (f32[384,96]{0,1:T(8,128)S(1)}, f32[384,96]{0,1:T(8,128)}, u32[]{:S(2)}) copy-start(f32[384,96]{0,1:T(8,128)} %param.11) | copy-start | bytes 442372
  10.3 483.5 %copy-start.7 = (f32[384,96]{0,1:T(8,128)S(1)}, f32[384,96]{0,1:T(8,128)}, u32[]{:S(2)}) copy-start(f32[384,96]{0,1:T(8,128)} %param.12) | copy-start | bytes 442372
  10.3 483.5 %copy-start.8 = (f32[384,96]{0,1:T(8,128)S(1)}, f32[384,96]{0,1:T(8,128)}, u32[]{:S(2)}) copy-start(f32[384,96]{0,1:T(8,128)} %param.13) | copy-start | bytes 442372
  10.3 529.1 %copy-start.10 = (f32[4,416]{1,0:T(4,128)S(1)}, f32[4,416]{1,0:T(4,128)}, u32[]{:S(2)}) copy-start(f32[4,416]{1,0:T(4,128)} %param.15) | copy-start | bytes 19972
  10.3 529.1 %copy-start.11 = (f32[4,416]{1,0:T(4,128)S(1)}, f32[4,416]{1,0:T(4,128)}, u32[]{:S(2)}) copy-start(f32[4,416]{1,0:T(4,128)} %param.16) | copy-start | bytes 19972
  10.3 529.1 %copy-start.12 = (f32[4,416]{1,0:T(4,128)S(1)}, f32[4,416]{1,0:T(4,128)}, u32[]{:S(2)}) copy-start(f32[4,416]{1,0:T(4,128)} %param.17) | copy-start | bytes 19972
  10.4 210.0 %all-reduce.2.cloned.1.call-start = ((), (), s32[]{:S(2)}) async-start(), calls=%async_computation.2 | async-start | bytes 294912 | tf_op jit(solution)/shard_map/psum | solution.py:50
  495.5 53.5 %copy-start = (f32[384,96]{0,1:T(8,128)}, f32[384,96]{0,1:T(8,128)S(1)}, u32[]{:S(2)}) copy-start(f32[384,96]{0,1:T(8,128)S(1)} %get-tuple-element.11) | copy-start | bytes 442372
  495.7 12.2 %collective-permute-start = (bf16[384,96]{1,0:T(8,128)(2,1)S(1)}, bf16[384,96]{1,0:T(8,128)(2,1)S(1)}, u32[]{:S(2)}, u32[]{:S(2)}) collective-permute-start(bf16[384,96]{1,0:T(8,128)(2,1)S(1)} %copy.18), channel_id=1, source_target_pairs={{0,8},{8,16},{16,24},{24,32},{32,40},{40,48},{48,56},{56,64},{64,7... | collective-permute-start | bytes 221192 | tf_op jit(solution)/shard_map/ppermute | solution.py:19
  495.7 12.4 %collective-permute-start.8 = (bf16[384,96]{1,0:T(8,128)(2,1)S(1)}, bf16[384,96]{1,0:T(8,128)(2,1)S(1)}, u32[]{:S(2)}, u32[]{:S(2)}) collective-permute-start(bf16[384,96]{1,0:T(8,128)(2,1)S(1)} %copy.18), channel_id=1, source_target_pairs={{0,120},{8,0},{16,8},{24,16},{32,24},{40,32},{48,40},{56,48},{64,5... | collective-permute-start | bytes 221192 | tf_op jit(solution)/shard_map/ppermute | solution.py:22
  507.9 5.2 collective-permute-start.1
  508.0 5.2 collective-permute-start.9
  513.1 5.3 collective-permute-start.2
  513.3 5.3 collective-permute-start.10
  518.4 5.3 collective-permute-start.3
  518.5 5.3 collective-permute-start.11
  523.6 5.3 collective-permute-start.4
  523.8 5.3 collective-permute-start.12
  528.9 5.3 collective-permute-start.5
  529.0 11.0 %copy-start.1 = (bf16[384,96]{1,0:T(8,128)(2,1)}, bf16[384,96]{1,0:T(8,128)(2,1)S(1)}, u32[]{:S(2)}) copy-start(bf16[384,96]{1,0:T(8,128)(2,1)S(1)} %collective-permute-done.12) | copy-start | bytes 221188
  529.0 5.3 collective-permute-start.13
  534.1 5.9 %copy-start.2 = (bf16[384,96]{1,0:T(8,128)(2,1)}, bf16[384,96]{1,0:T(8,128)(2,1)S(1)}, u32[]{:S(2)}) copy-start(bf16[384,96]{1,0:T(8,128)(2,1)S(1)} %collective-permute-done.5) | copy-start | bytes 221188
  534.1 5.3 collective-permute-start.6
  534.3 5.8 %copy-start.3 = (bf16[384,96]{1,0:T(8,128)(2,1)}, bf16[384,96]{1,0:T(8,128)(2,1)S(1)}, u32[]{:S(2)}) copy-start(bf16[384,96]{1,0:T(8,128)(2,1)S(1)} %collective-permute-done.13) | copy-start | bytes 221188
  534.3 5.8 %collective-permute-start.14 = (bf16[384,96]{1,0:T(8,128)(2,1)S(1)}, bf16[384,96]{1,0:T(8,128)(2,1)S(1)}, u32[]{:S(2)}, u32[]{:S(2)}) collective-permute-start(bf16[384,96]{1,0:T(8,128)(2,1)S(1)} %collective-permute-done.13), channel_id=1, source_target_pairs={{0,120},{8,0},{16,8},{24,16},{32,24},{40,32},{48,40},{56,48},{64,5... | collective-permute-start | bytes 221192 | tf_op jit(solution)/shard_map/ppermute | solution.py:22
  539.4 0.7 copy-start.4
  539.4 5.4 collective-permute-start.7
  540.1 0.6 copy-start.5
  549.0 1.6 copy-start.9
Sparse Core Ops, SparseCore 0:
  10.8 65.6 reduce-scatter.1
  79.4 54.9 all-reduce.1
